TPU v7x, 32 devices: a whole 2x2x4 slice. The times are simulated.
32 devices in a mesh: roll: 4 (over y, x), seq: 8 (over z, core).
Axes of the slice: x: 2, y: 2, z: 4, core: 2. Of those that a mesh axis runs over, the one named last changes fastest.
Arguments:
- query_rows: bfloat16 [4, 4096, 1792], P('roll', 'seq'), may hold values from -200 to 200
- key_rows: bfloat16 [4, 4096, 256], P('roll', 'seq'), may hold values from -6 to 6
- value_rows: bfloat16 [4, 4096, 256], P('roll', 'seq'), may hold values from -6 to 6
- cotangent: bfloat16 [4, 4096, 1792], P('roll', None, 'seq'), may hold values from -6 to 6
- slopes: float32 [14], replicated, may hold values from 0.00029296876 to 0.0390625
- lengths: int32 [4], P('roll'), may hold values from 1024 to 4096, as said below
- loss_mask: int32 [4, 4096], P('roll', 'seq'), may hold values 0 or 1
- distances: int32 [4], P('roll'), may hold values from 40 to 357
Outputs:
- grad_queries: bfloat16 [4, 4096, 1792], P('roll', 'seq')
- grad_keys: bfloat16 [4, 4096, 256], P('roll', 'seq')
- grad_values: bfloat16 [4, 4096, 256], P('roll', 'seq')
Inputs may be any that keep to these rules, and one draw needn't show every extreme that they name: `lengths`: some rollout has 4096 tokens and some 4096 // 4.
All inputs are finite; a program needn't handle non-finite values. No bound on the sum of `loss_mask` on one device may be relied on, other than what follows from the above.
Results may differ from a plain program's by a relative error of at most 0.0068.
Values may be sent and summed in bfloat16 or wider, within the bound.
No kernel may reach another device: no remote copies, remote signals or barrier semaphores. Data moves between devices by JAX's collectives and lax.ppermute only.
A program may use at most 64 MiB of HBM per device.

v0:
```python
import math
import jax
import jax.numpy as jnp
from jax import lax
from jax.sharding import PartitionSpec as P

HEAD_DIM = 128
WINDOW = 1024


def passed_along(value, axis, steps):
    count = lax.axis_size(axis)
    leading, last = (max(0, -steps), min(count, count - steps))
    return lax.ppermute(value, axis, [(source, source + steps) for source in range(leading, last)])


def shards(query_rows, key_rows, value_rows, cotangent, slopes, lengths, loss_mask, distances):
    own_q = query_rows[0]
    own_k = key_rows[0]
    own_v = value_rows[0]
    tok_rows = own_q.shape[0]
    features = own_q.shape[1]
    kv_features = own_k.shape[1]
    head_dim = HEAD_DIM
    head_count = features // head_dim
    kv_count = kv_features // head_dim
    group_size = head_count // kv_count
    band_reach = (WINDOW - 2) // tok_rows + 1
    band_len = (band_reach + 1) * tok_rows
    seq_len = tok_rows * lax.axis_size("seq")
    seq_pos = lax.axis_index("seq")
    attn_scale = 1.0 / math.sqrt(head_dim)
    positions = seq_pos * tok_rows + jnp.arange(tok_rows, dtype=jnp.int32)
    valid = ((positions < lengths[0]) & (loss_mask[0] == 1)).astype(jnp.float32)
    local_count = jnp.sum(valid)
    my_distance = distances[0].astype(jnp.float32)
    count_all = lax.psum(local_count, "seq")
    group_total = lax.psum(my_distance, "roll")
    advantage = (group_total / lax.axis_size("roll") - my_distance) / 64.0
    weight = advantage * valid * seq_len / (1.0 + count_all)
    arrived = lax.all_to_all(cotangent, "seq", split_axis=1, concat_axis=2, tiled=True)[0]
    dout = (arrived.astype(jnp.float32) * weight[:, None]).astype(jnp.bfloat16)
    kv_pair = jnp.stack([own_k, own_v])
    earlier = []
    for offset in range(1, band_reach + 1):
        earlier.append(passed_along(kv_pair, "seq", offset))
    ordered = earlier[::-1]
    band_k = jnp.concatenate([blk[0] for blk in ordered] + [own_k], 0)
    band_v = jnp.concatenate([blk[1] for blk in ordered] + [own_v], 0)
    key_pos = (seq_pos - band_reach) * tok_rows + jnp.arange(band_len, dtype=jnp.int32)
    pos_gap = positions[:, None] - key_pos[None, :]
    allowed = (pos_gap >= 0) & (pos_gap < WINDOW) & (key_pos[None, :] >= 0)
    gap_float = pos_gap.astype(jnp.float32)
    split_at = band_reach * tok_rows
    contract_rows = (((0,), (0,)), ((), ()))

    def head_step(head, carry):
        grad_q, own_dk, own_dv, part_k, part_v = carry
        column = head * head_dim
        kv_column = head // group_size * head_dim
        q_head = lax.dynamic_slice_in_dim(own_q, column, head_dim, 1)
        k_head = lax.dynamic_slice_in_dim(band_k, kv_column, head_dim, 1)
        v_head = lax.dynamic_slice_in_dim(band_v, kv_column, head_dim, 1)
        d_head = lax.dynamic_slice_in_dim(dout, column, head_dim, 1)
        slope = lax.dynamic_index_in_dim(slopes, head, keepdims=False)
        scores = (
            jnp.dot(q_head, k_head.T, preferred_element_type=jnp.float32) * attn_scale
            - slope * gap_float
        )
        masked = jnp.where(allowed, scores, -jnp.inf)
        row_max = jnp.max(masked, axis=1, keepdims=True)
        exp_terms = jnp.where(allowed, jnp.exp(masked - row_max), 0.0)
        probs = exp_terms / jnp.sum(exp_terms, axis=1, keepdims=True)
        probs_low = probs.astype(jnp.bfloat16)
        dprob = jnp.dot(d_head, v_head.T, preferred_element_type=jnp.float32)
        row_delta = jnp.sum(probs * dprob, axis=1, keepdims=True)
        dscore = (probs * (dprob - row_delta) * attn_scale).astype(jnp.bfloat16)
        head_dq = jnp.dot(dscore, k_head, preferred_element_type=jnp.float32).astype(jnp.bfloat16)
        band_dk = lax.dot_general(dscore, q_head, contract_rows, preferred_element_type=jnp.float32)
        band_dv = lax.dot_general(
            probs_low, d_head, contract_rows, preferred_element_type=jnp.float32
        )
        grad_q = lax.dynamic_update_slice_in_dim(grad_q, head_dq, column, 1)
        own_dk = lax.dynamic_update_slice_in_dim(
            own_dk,
            lax.dynamic_slice_in_dim(own_dk, kv_column, head_dim, 1) + band_dk[split_at:],
            kv_column,
            1,
        )
        own_dv = lax.dynamic_update_slice_in_dim(
            own_dv,
            lax.dynamic_slice_in_dim(own_dv, kv_column, head_dim, 1) + band_dv[split_at:],
            kv_column,
            1,
        )
        far_dk = band_dk[:split_at].reshape(band_reach, tok_rows, head_dim)
        far_dv = band_dv[:split_at].reshape(band_reach, tok_rows, head_dim)
        part_k = lax.dynamic_update_slice_in_dim(
            part_k, lax.dynamic_slice_in_dim(part_k, kv_column, head_dim, 2) + far_dk, kv_column, 2
        )
        part_v = lax.dynamic_update_slice_in_dim(
            part_v, lax.dynamic_slice_in_dim(part_v, kv_column, head_dim, 2) + far_dv, kv_column, 2
        )
        return (grad_q, own_dk, own_dv, part_k, part_v)

    start_carry = (
        jnp.zeros((tok_rows, features), jnp.bfloat16),
        jnp.zeros((tok_rows, kv_features), jnp.float32),
        jnp.zeros((tok_rows, kv_features), jnp.float32),
        jnp.zeros((band_reach, tok_rows, kv_features), jnp.float32),
        jnp.zeros((band_reach, tok_rows, kv_features), jnp.float32),
    )
    grad_q, total_k, total_v, part_k, part_v = lax.fori_loop(0, head_count, head_step, start_carry)
    part_k = part_k.astype(jnp.bfloat16)
    part_v = part_v.astype(jnp.bfloat16)
    for offset in range(1, band_reach + 1):
        outgoing = jnp.stack([part_k[band_reach - offset], part_v[band_reach - offset]])
        incoming = passed_along(outgoing, "seq", -offset)
        total_k = total_k + incoming[0].astype(jnp.float32)
        total_v = total_v + incoming[1].astype(jnp.float32)
    return (grad_q[None], total_k.astype(jnp.bfloat16)[None], total_v.astype(jnp.bfloat16)[None])


def solution(mesh):
    placed = (
        P("roll", "seq", None),
        P("roll", "seq", None),
        P("roll", "seq", None),
        P("roll", None, "seq"),
        P(),
        P("roll"),
        P("roll", "seq"),
        P("roll"),
    )
    return jax.shard_map(
        shards,
        mesh=mesh,
        in_specs=placed,
        out_specs=(P("roll", "seq", None), P("roll", "seq", None), P("roll", "seq", None)),
        check_vma=False,
    )
```

profile of v0, /device:TPU:19, one launch (start us, length us, event | category | flops | bytes accessed | tf_op | source)
XLA Modules:
  0.0 346.7 jit_solution(13123298232539514425)
XLA Ops:
  0.6 10.0 %copy.19 = bf16[1,4096,224]{2,0,1:T(2,128)(2,1)} copy(bf16[1,4096,224]{1,2,0:T(8,128)(2,1)} %param.13) | data formatting | bytes 3670016 | tf_op args[3]
  11.1 23.6 %reduce.2 = bf16[4096,224]{1,0:T(8,128)(2,1)S(1)} reduce(bf16[4096,1,224]{2,1,0:T(2,128)(2,1)} %bitcast.71, bf16[]{:T(256)} %broadcast.76), dimensions={1}, to_apply=%bitcast.53.reduce_sub_computation | reduce | bytes 3670018
  34.8 5.2 %reshape.80 = bf16[8,2,57344]{2,1,0:T(2,128)(2,1)} reshape(bf16[4096,224]{1,0:T(8,128)(2,1)S(1)} %reduce.2) | data formatting | bytes 3670016
  40.0 5.7 %all-to-all-start = ((bf16[8,2,57344]{2,1,0:T(2,128)(2,1)}), bf16[8,2,57344]{2,1,0:T(2,128)(2,1)S(1)}, u32[]{:S(2)}, u32[]{:S(2)}) async-start(bf16[8,2,57344]{2,1,0:T(2,128)(2,1)} %reshape.80), calls=%async_computation | async-start | bytes 3670016 | tf_op jit(solution)/shard_map/all_to_all | solution.py:41
  47.1 3.3 collective-permute-start.1
  50.4 1.9 collective-permute-start
  54.3 7.8 %psum.14 = f32[]{:T(128)} all-reduce(f32[]{:T(128)} %bitcast.7), channel_id=1, replica_groups=mesh['roll'=4,'seq'=8] {'roll'}, use_global_device_ids=true, to_apply=%region_0.0 | all-reduce | flops 1 | bytes 8 | tf_op jit(solution)/shard_map/psum | solution.py:38
  62.0 47.4 %psum.15 = f32[]{:T(128)} all-reduce(f32[]{:T(128)} %convert_reduce_fusion), channel_id=1, replica_groups=mesh['roll'=4,'seq'=8] {'seq'}, use_global_device_ids=true, to_apply=%region_2.0 | all-reduce | flops 1 | bytes 8 | tf_op jit(solution)/shard_map/psum | solution.py:37
  113.1 5.8 %reshape.81 = bf16[4096,1,224]{2,1,0:T(2,128)(2,1)} reshape(bf16[8,2,57344]{2,1,0:T(2,128)(2,1)S(1)} %all-to-all-done) | data formatting | bytes 3670016
  118.9 10.1 %copy.20 = bf16[1,4096,224]{1,2,0:T(8,128)(2,1)S(1)} copy(bf16[1,4096,224]{2,0,1:T(2,128)(2,1)} %bitcast.72) | data formatting | bytes 3670016 | tf_op jit(solution)/shard_map/all_to_all | solution.py:41
  129.5 3.3 copy.24
  132.7 2.1 copy.21
  134.9 1.8 fusion.30
  138.3 186.0 %while.25 = (s32[]{:T(128)}, bf16[512,1792]{1,0:T(8,128)(2,1)}, f32[512,256]{1,0:T(8,128)S(1)}, f32[512,256]{1,0:T(8,128)S(1)}, f32[2,512,256]{2,1,0:T(8,128)S(1...) while((s32[]{:T(128)}, bf16[512,1792]{1,0:T(8,128)(2,1)}, ...), condition=%wide.region_7.8_spmd.clone.clone, body=%wide.region_3.7_spmd.clone.clone.sunk | while | flops 1033828864 | bytes 46446556 | solution.py:113
  138.8 3.3 fusion.59
  143.5 2.8 multiply_reduce_fusion.2
  152.1 3.3 fusion.59
  156.8 2.8 multiply_reduce_fusion.2
  165.4 3.3 fusion.59
  170.0 2.8 multiply_reduce_fusion.2
  178.6 3.3 fusion.59
  183.3 2.8 multiply_reduce_fusion.2
  191.9 3.3 fusion.59
  196.6 2.8 multiply_reduce_fusion.2
  205.2 3.3 fusion.59
  209.8 2.8 multiply_reduce_fusion.2
  218.4 3.3 fusion.59
  223.1 2.8 multiply_reduce_fusion.2
  231.7 3.3 fusion.59
  236.3 2.8 multiply_reduce_fusion.2
  239.6 1.6 fusion.62
  245.0 3.3 fusion.59
  249.7 2.8 multiply_reduce_fusion.2
  252.9 1.6 fusion.62
  258.3 3.3 fusion.59
  263.0 2.8 multiply_reduce_fusion.2
  271.7 3.3 fusion.59
  276.3 2.8 multiply_reduce_fusion.2
  285.0 3.3 fusion.59
  289.6 2.8 multiply_reduce_fusion.2
  298.3 3.3 fusion.59
  303.0 2.8 multiply_reduce_fusion.2
  311.6 3.3 fusion.59
  316.3 2.8 multiply_reduce_fusion.2
  324.6 1.9 collective-permute-start.3
  326.6 2.1 collective-permute-start.2
  328.7 11.2 %collective-permute-done.3 = bf16[2,512,256]{2,1,0:T(8,128)(2,1)S(1)} collective-permute-done((bf16[2,512,256]{2,1,0:T(8,128)(2,1)S(1)}, bf16[2,512,256]{2,1,0:T(8,128)(2,1)S(1)}, u32[]{:S(2)}, u32[]{:S(2)}) %collective-permute-start.3) | collective-permute-done | bytes 524320 | tf_op jit(solution)/shard_map/ppermute | solution.py:14
  339.9 5.9 %collective-permute-done.2 = bf16[2,512,256]{2,1,0:T(8,128)(2,1)S(1)} collective-permute-done((bf16[2,512,256]{2,1,0:T(8,128)(2,1)S(1)}, bf16[2,512,256]{2,1,0:T(8,128)(2,1)S(1)}, u32[]{:S(2)}, u32[]{:S(2)}) %collective-permute-start.2) | collective-permute-done | bytes 524320 | tf_op jit(solution)/shard_map/ppermute | solution.py:14
  (230 shorter events, 104.8 us)
Async XLA Ops:
  34.7 10.9 %copy-start.1 = (bf16[1,512,256]{2,1,0:T(8,128)(2,1)S(1)}, bf16[1,512,256]{2,1,0:T(8,128)(2,1)}, u32[]{:S(2)}) copy-start(bf16[1,512,256]{2,1,0:T(8,128)(2,1)} %param.11) | copy-start | bytes 786436
  34.8 11.6 %copy-start.2 = (bf16[1,512,256]{2,1,0:T(8,128)(2,1)S(1)}, bf16[1,512,256]{2,1,0:T(8,128)(2,1)}, u32[]{:S(2)}) copy-start(bf16[1,512,256]{2,1,0:T(8,128)(2,1)} %param.12) | copy-start | bytes 786436
  40.0 13.7 %copy-start.4 = (s32[1,512]{1,0:T(1,128)S(1)}, s32[1,512]{1,0:T(1,128)}, u32[]{:S(2)}) copy-start(s32[1,512]{1,0:T(1,128)} %param.16) | copy-start | bytes 6148
  40.0 73.2 %all-to-all-start = ((bf16[8,2,57344]{2,1,0:T(2,128)(2,1)}), bf16[8,2,57344]{2,1,0:T(2,128)(2,1)S(1)}, u32[]{:S(2)}, u32[]{:S(2)}) async-start(bf16[8,2,57344]{2,1,0:T(2,128)(2,1)} %reshape.80), calls=%async_computation | async-start | bytes 3670016 | tf_op jit(solution)/shard_map/all_to_all | solution.py:41
  47.1 63.7 %collective-permute-start.1 = (bf16[2,512,256]{2,1,0:T(8,128)(2,1)}, bf16[2,512,256]{2,1,0:T(8,128)(2,1)}, u32[]{:S(2)}, u32[]{:S(2)}) collective-permute-start(bf16[2,512,256]{2,1,0:T(8,128)(2,1)} %constant_dynamic-update-slice_fusion), channel_id=1, source_target_pairs={{0,1},{1,2},{2,3},{3,4},{4,5},{5,6},{6,7},{8,9},{9,10},{10,11},{11... | collective-permute-start | bytes 1572872 | tf_op jit(solution)/shard_map/ppermute | solution.py:14
  50.4 61.4 %collective-permute-start = (bf16[2,512,256]{2,1,0:T(8,128)(2,1)}, bf16[2,512,256]{2,1,0:T(8,128)(2,1)S(1)}, u32[]{:S(2)}, u32[]{:S(2)}) collective-permute-start(bf16[2,512,256]{2,1,0:T(8,128)(2,1)} %constant_dynamic-update-slice_fusion), channel_id=1, source_target_pairs={{0,2},{1,3},{2,4},{3,5},{4,6},{5,7},{8,10},{9,11},{10,12},{11,13},... | collective-permute-start | bytes 1572872 | tf_op jit(solution)/shard_map/ppermute | solution.py:14
  136.7 1.6 copy-start.5
  142.1 1.4 copy-start.3
  146.7 3.2 copy-start
  155.4 1.4 copy-start.3
  160.0 3.2 copy-start
  168.6 1.4 copy-start.3
  173.2 3.2 copy-start
  181.9 1.4 copy-start.3
  186.5 3.2 copy-start
  195.2 1.4 copy-start.3
  199.8 3.2 copy-start
  208.4 1.4 copy-start.3
  213.0 3.2 copy-start
  221.7 1.4 copy-start.3
  226.3 3.2 copy-start
  235.0 1.4 copy-start.3
  239.6 3.2 copy-start
  248.3 1.4 copy-start.3
  252.9 3.2 copy-start
  261.6 1.4 copy-start.3
  266.2 3.2 copy-start
  274.9 1.4 copy-start.3
  279.5 3.2 copy-start
  288.3 1.4 copy-start.3
  292.8 3.2 copy-start
  301.6 1.4 copy-start.3
  306.2 3.2 copy-start
  314.9 1.4 copy-start.3
  319.5 3.2 copy-start
  324.6 15.3 %collective-permute-start.3 = (bf16[2,512,256]{2,1,0:T(8,128)(2,1)S(1)}, bf16[2,512,256]{2,1,0:T(8,128)(2,1)S(1)}, u32[]{:S(2)}, u32[]{:S(2)}) collective-permute-start(bf16[2,512,256]{2,1,0:T(8,128)(2,1)S(1)} %pad_maximum_fusion.3), channel_id=1, source_target_pairs={{2,0},{3,1},{4,2},{5,3},{6,4},{7,5},{10,8},{11,9},{12,10},{13,11},... | collective-permute-start | bytes 1572872 | tf_op jit(solution)/shard_map/ppermute | solution.py:14
  326.6 19.2 %collective-permute-start.2 = (bf16[2,512,256]{2,1,0:T(8,128)(2,1)S(1)}, bf16[2,512,256]{2,1,0:T(8,128)(2,1)S(1)}, u32[]{:S(2)}, u32[]{:S(2)}) collective-permute-start(bf16[2,512,256]{2,1,0:T(8,128)(2,1)S(1)} %pad_maximum_fusion.2), channel_id=1, source_target_pairs={{1,0},{2,1},{3,2},{4,3},{5,4},{6,5},{7,6},{9,8},{10,9},{11,10},{12... | collective-permute-start | bytes 1572872 | tf_op jit(solution)/shard_map/ppermute | solution.py:14
where the time goes:
time: 349 us; the launch traced here: 347 us
  matrix products  146 us (42%)
  other arithmetic  58.4 us (17%)
  blocking collectives  55.2 us (16%)
  local copies, waits for them, and re-layouts  50.5 us (14%)
  waiting for transfers between devices  17.1 us (5%)
  starting transfers between devices  14.9 us (4%)
    psum x1, blocking collectives, shards(): count_all = lax.psum(local_count, 'seq')  47.4 us
    dot_general x14, matrix products, head_step(): jnp.dot(q_head, k_head.T, preferred_element_type=jnp.float32) * attn_scale  45.8 us
    dot_general x14, matrix products, head_step(): dprob = jnp.dot(d_head, v_head.T, preferred_element_type=jnp.float32)  38.8 us
    unnamed x14, local copies, waits for them, and re-layouts  25.4 us
    unnamed x1, other arithmetic  23.6 us
    dot_general x14, matrix products, head_step(): lax.dot_general(probs_low, d_head, contract_rows, preferred_element_type=...  22.3 us
    dot_general x14, matrix products, head_step(): lax.dot_general(dscore, q_head, contract_rows, preferred_element_type=jnp...  21.3 us
    reduce_sum x14, other arithmetic, head_step(): probs = exp_terms / jnp.sum(exp_terms, axis=1, keepdims=True)  19.1 us
  transfers between devices with their start and end apart: 5, of which 2 were waited for; matrix products, arithmetic and copies ran while one was open for 1% of the time, Pallas kernels for 0%

commit v1 on v0

--- a/solution.py
+++ b/solution.py
@@ -38,7 +38,10 @@
     group_total = lax.psum(my_distance, "roll")
     advantage = (group_total / lax.axis_size("roll") - my_distance) / 64.0
     weight = advantage * valid * seq_len / (1.0 + count_all)
-    arrived = lax.all_to_all(cotangent, "seq", split_axis=1, concat_axis=2, tiled=True)[0]
+    arrived = jnp.concatenate(
+        lax.all_to_all(jnp.stack(jnp.split(cotangent, lax.axis_size("seq"), axis=1)), "seq", 0, 0),
+        axis=2,
+    )[0]
     dout = (arrived.astype(jnp.float32) * weight[:, None]).astype(jnp.bfloat16)
     kv_pair = jnp.stack([own_k, own_v])
     earlier = []

time: 349 us -> 300 us (0.86)
  local copies, waits for them, and re-layouts: 50.5 us -> 25.6 us
  other arithmetic: 58.4 us -> 34.8 us
    unnamed x1 -> x0, other arithmetic: 23.6 us -> none
    unnamed x14 -> x16, local copies, waits for them, and re-layouts: 25.4 us -> 12.2 us
    all_to_all x1 -> x0, local copies, waits for them, and re-layouts: 10.1 us -> none  [shards(): lax.all_to_all(cotangent, 'seq', split_axis=1, concat_axis=2, tiled=True)[0]]
where the time goes in v1:
time: 300 us; the launch traced here: 298 us
  matrix products  146 us (49%)
  blocking collectives  55.2 us (18%)
  other arithmetic  34.8 us (12%)
  local copies, waits for them, and re-layouts  25.6 us (9%)
  waiting for transfers between devices  17.1 us (6%)
  starting transfers between devices  14.9 us (5%)
  between operations  3.38 us (1%)
    psum x1, blocking collectives, shards(): count_all = lax.psum(local_count, 'seq')  47.4 us
    dot_general x14, matrix products, head_step(): jnp.dot(q_head, k_head.T, preferred_element_type=jnp.float32) * attn_scale  45.8 us
    dot_general x14, matrix products, head_step(): dprob = jnp.dot(d_head, v_head.T, preferred_element_type=jnp.float32)  38.8 us
    dot_general x14, matrix products, head_step(): lax.dot_general(dscore, q_head, contract_rows, preferred_element_type=jnp...  22.2 us
    dot_general x14, matrix products, head_step(): lax.dot_general(probs_low, d_head, contract_rows, preferred_element_type=...  21.3 us
    reduce_sum x14, other arithmetic, head_step(): probs = exp_terms / jnp.sum(exp_terms, axis=1, keepdims=True)  19.1 us
    dot_general x14, matrix products, head_step(): jnp.dot(dscore, k_head, preferred_element_type=jnp.float32)  17.4 us
    ppermute x4, waiting for transfers between devices, passed_along(): lax.ppermute(value, axis, [(source, source + steps) for source in range(l...  17.1 us
  transfers between devices with their start and end apart: 5, of which 2 were waited for; matrix products, arithmetic and copies ran while one was open for 1% of the time, Pallas kernels for 0%

profile of v1, /device:TPU:19, one launch (start us, length us, event | category | flops | bytes accessed | tf_op | source)
XLA Modules:
  0.0 298.2 jit_solution(8794540132780528772)
XLA Ops:
  0.6 1.6 bitcast_dynamic-update-slice_fusion.7
  2.3 1.6 bitcast_dynamic-update-slice_fusion.6
  3.9 1.6 bitcast_dynamic-update-slice_fusion.5
  5.6 1.6 bitcast_dynamic-update-slice_fusion.4
  7.2 1.6 bitcast_dynamic-update-slice_fusion.3
  8.8 1.6 bitcast_dynamic-update-slice_fusion.2
  10.5 1.6 bitcast_dynamic-update-slice_fusion.1
  12.1 1.6 bitcast_dynamic-update-slice_fusion
  13.8 5.7 %all-to-all-start = ((bf16[8,1,512,224]{2,3,1,0:T(8,128)(2,1)}), bf16[8,1,512,224]{2,3,1,0:T(8,128)(2,1)S(1)}, u32[]{:S(2)}, u32[]{:S(2)}) async-start(bf16[8,1,512,224]{2,3,1,0:T(8,128)(2,1)} %bitcast_dynamic-update-slice_fusion), calls=%async_computation | async-start | bytes 3670016 | tf_op jit(solution)/shard_map/all_to_all | solution.py:42
  20.9 3.3 %collective-permute-start.1 = (bf16[2,512,256]{2,1,0:T(8,128)(2,1)}, bf16[2,512,256]{2,1,0:T(8,128)(2,1)S(1)}, u32[]{:S(2)}, u32[]{:S(2)}) collective-permute-start(bf16[2,512,256]{2,1,0:T(8,128)(2,1)} %constant_dynamic-update-slice_fusion), channel_id=1, source_target_pairs={{0,1},{1,2},{2,3},{3,4},{4,5},{5,6},{6,7},{8,9},{9,10},{10,11},{11... | collective-permute-start | bytes 1572872 | tf_op jit(solution)/shard_map/ppermute | solution.py:14
  24.2 1.9 collective-permute-start
  28.1 7.8 %psum.14 = f32[]{:T(128)} all-reduce(f32[]{:T(128)} %bitcast.16), channel_id=1, replica_groups=mesh['roll'=4,'seq'=8] {'roll'}, use_global_device_ids=true, to_apply=%region_0.0 | all-reduce | flops 1 | bytes 8 | tf_op jit(solution)/shard_map/psum | solution.py:38
  35.9 47.4 %psum.15 = f32[]{:T(128)} all-reduce(f32[]{:T(128)} %convert_reduce_fusion), channel_id=1, replica_groups=mesh['roll'=4,'seq'=8] {'seq'}, use_global_device_ids=true, to_apply=%region_2.0 | all-reduce | flops 1 | bytes 8 | tf_op jit(solution)/shard_map/psum | solution.py:37
  86.4 1.8 fusion.30
  89.8 186.0 %while.25 = (s32[]{:T(128)}, bf16[512,1792]{1,0:T(8,128)(2,1)}, f32[512,256]{1,0:T(8,128)S(1)}, f32[512,256]{1,0:T(8,128)S(1)}, f32[2,512,256]{2,1,0:T(8,128)S(1...) while((s32[]{:T(128)}, bf16[512,1792]{1,0:T(8,128)(2,1)}, ...), condition=%wide.region_7.8_spmd.clone.clone, body=%wide.region_3.7_spmd.clone.clone.sunk | while | flops 1033828864 | bytes 46446556 | solution.py:116
  90.4 3.3 %fusion.59 = (f32[512]{0:T(512)S(1)}, f32[512,1536]{1,0:T(8,128)S(1)}) fusion(f32[]{:T(128)} %bitcast.74, bf16[1536,256]{1,0:T(8,128)(2,1)} %get-tuple-element.625, s32[]{:T(128)S(6)} %select_n.97, bf16[512,1792]{1,0:T(8,128)(2,1)} %get-tuple-element.624, s32[]{:T(128)S(6)} %select_n.95, pred[1536]{0:T(1024)(128)(4,1)S(1)} %get-tuple-element.631, ...), kind=kOutput, calls=%fused_computation.80.clone.1 | convolution fusion | flops 209976832 | bytes 3682312 | tf_op jit(solution)/shard_map/while/body/eval_jaxpr/dot_general | solution.py:70
  95.1 2.8 multiply_reduce_fusion.2
  103.7 3.3 %fusion.59 = (f32[512]{0:T(512)S(1)}, f32[512,1536]{1,0:T(8,128)S(1)}) fusion(f32[]{:T(128)} %bitcast.74, bf16[1536,256]{1,0:T(8,128)(2,1)} %get-tuple-element.625, s32[]{:T(128)S(6)} %select_n.97, bf16[512,1792]{1,0:T(8,128)(2,1)} %get-tuple-element.624, s32[]{:T(128)S(6)} %select_n.95, pred[1536]{0:T(1024)(128)(4,1)S(1)} %get-tuple-element.631, ...), kind=kOutput, calls=%fused_computation.80.clone.1 | convolution fusion | flops 209976832 | bytes 3682312 | tf_op jit(solution)/shard_map/while/body/eval_jaxpr/dot_general | solution.py:70
  108.3 2.8 multiply_reduce_fusion.2
  113.1 1.6 fusion.63
  116.9 3.3 %fusion.59 = (f32[512]{0:T(512)S(1)}, f32[512,1536]{1,0:T(8,128)S(1)}) fusion(f32[]{:T(128)} %bitcast.74, bf16[1536,256]{1,0:T(8,128)(2,1)} %get-tuple-element.625, s32[]{:T(128)S(6)} %select_n.97, bf16[512,1792]{1,0:T(8,128)(2,1)} %get-tuple-element.624, s32[]{:T(128)S(6)} %select_n.95, pred[1536]{0:T(1024)(128)(4,1)S(1)} %get-tuple-element.631, ...), kind=kOutput, calls=%fused_computation.80.clone.1 | convolution fusion | flops 209976832 | bytes 3682312 | tf_op jit(solution)/shard_map/while/body/eval_jaxpr/dot_general | solution.py:70
  121.6 2.8 multiply_reduce_fusion.2
  130.2 3.3 %fusion.59 = (f32[512]{0:T(512)S(1)}, f32[512,1536]{1,0:T(8,128)S(1)}) fusion(f32[]{:T(128)} %bitcast.74, bf16[1536,256]{1,0:T(8,128)(2,1)} %get-tuple-element.625, s32[]{:T(128)S(6)} %select_n.97, bf16[512,1792]{1,0:T(8,128)(2,1)} %get-tuple-element.624, s32[]{:T(128)S(6)} %select_n.95, pred[1536]{0:T(1024)(128)(4,1)S(1)} %get-tuple-element.631, ...), kind=kOutput, calls=%fused_computation.80.clone.1 | convolution fusion | flops 209976832 | bytes 3682312 | tf_op jit(solution)/shard_map/while/body/eval_jaxpr/dot_general | solution.py:70
  134.8 2.8 multiply_reduce_fusion.2
  143.4 3.3 %fusion.59 = (f32[512]{0:T(512)S(1)}, f32[512,1536]{1,0:T(8,128)S(1)}) fusion(f32[]{:T(128)} %bitcast.74, bf16[1536,256]{1,0:T(8,128)(2,1)} %get-tuple-element.625, s32[]{:T(128)S(6)} %select_n.97, bf16[512,1792]{1,0:T(8,128)(2,1)} %get-tuple-element.624, s32[]{:T(128)S(6)} %select_n.95, pred[1536]{0:T(1024)(128)(4,1)S(1)} %get-tuple-element.631, ...), kind=kOutput, calls=%fused_computation.80.clone.1 | convolution fusion | flops 209976832 | bytes 3682312 | tf_op jit(solution)/shard_map/while/body/eval_jaxpr/dot_general | solution.py:70
  148.1 2.8 multiply_reduce_fusion.2
  156.7 3.3 %fusion.59 = (f32[512]{0:T(512)S(1)}, f32[512,1536]{1,0:T(8,128)S(1)}) fusion(f32[]{:T(128)} %bitcast.74, bf16[1536,256]{1,0:T(8,128)(2,1)} %get-tuple-element.625, s32[]{:T(128)S(6)} %select_n.97, bf16[512,1792]{1,0:T(8,128)(2,1)} %get-tuple-element.624, s32[]{:T(128)S(6)} %select_n.95, pred[1536]{0:T(1024)(128)(4,1)S(1)} %get-tuple-element.631, ...), kind=kOutput, calls=%fused_computation.80.clone.1 | convolution fusion | flops 209976832 | bytes 3682312 | tf_op jit(solution)/shard_map/while/body/eval_jaxpr/dot_general | solution.py:70
  161.3 2.8 multiply_reduce_fusion.2
  169.9 3.3 %fusion.59 = (f32[512]{0:T(512)S(1)}, f32[512,1536]{1,0:T(8,128)S(1)}) fusion(f32[]{:T(128)} %bitcast.74, bf16[1536,256]{1,0:T(8,128)(2,1)} %get-tuple-element.625, s32[]{:T(128)S(6)} %select_n.97, bf16[512,1792]{1,0:T(8,128)(2,1)} %get-tuple-element.624, s32[]{:T(128)S(6)} %select_n.95, pred[1536]{0:T(1024)(128)(4,1)S(1)} %get-tuple-element.631, ...), kind=kOutput, calls=%fused_computation.80.clone.1 | convolution fusion | flops 209976832 | bytes 3682312 | tf_op jit(solution)/shard_map/while/body/eval_jaxpr/dot_general | solution.py:70
  174.6 2.8 multiply_reduce_fusion.2
  183.2 3.3 %fusion.59 = (f32[512]{0:T(512)S(1)}, f32[512,1536]{1,0:T(8,128)S(1)}) fusion(f32[]{:T(128)} %bitcast.74, bf16[1536,256]{1,0:T(8,128)(2,1)} %get-tuple-element.625, s32[]{:T(128)S(6)} %select_n.97, bf16[512,1792]{1,0:T(8,128)(2,1)} %get-tuple-element.624, s32[]{:T(128)S(6)} %select_n.95, pred[1536]{0:T(1024)(128)(4,1)S(1)} %get-tuple-element.631, ...), kind=kOutput, calls=%fused_computation.80.clone.1 | convolution fusion | flops 209976832 | bytes 3682312 | tf_op jit(solution)/shard_map/while/body/eval_jaxpr/dot_general | solution.py:70
  187.8 2.8 multiply_reduce_fusion.2
  196.5 3.3 %fusion.59 = (f32[512]{0:T(512)S(1)}, f32[512,1536]{1,0:T(8,128)S(1)}) fusion(f32[]{:T(128)} %bitcast.74, bf16[1536,256]{1,0:T(8,128)(2,1)} %get-tuple-element.625, s32[]{:T(128)S(6)} %select_n.97, bf16[512,1792]{1,0:T(8,128)(2,1)} %get-tuple-element.624, s32[]{:T(128)S(6)} %select_n.95, pred[1536]{0:T(1024)(128)(4,1)S(1)} %get-tuple-element.631, ...), kind=kOutput, calls=%fused_computation.80.clone.1 | convolution fusion | flops 209976832 | bytes 3682312 | tf_op jit(solution)/shard_map/while/body/eval_jaxpr/dot_general | solution.py:70
  201.2 2.8 multiply_reduce_fusion.2
  209.8 3.3 %fusion.59 = (f32[512]{0:T(512)S(1)}, f32[512,1536]{1,0:T(8,128)S(1)}) fusion(f32[]{:T(128)} %bitcast.74, bf16[1536,256]{1,0:T(8,128)(2,1)} %get-tuple-element.625, s32[]{:T(128)S(6)} %select_n.97, bf16[512,1792]{1,0:T(8,128)(2,1)} %get-tuple-element.624, s32[]{:T(128)S(6)} %select_n.95, pred[1536]{0:T(1024)(128)(4,1)S(1)} %get-tuple-element.631, ...), kind=kOutput, calls=%fused_computation.80.clone.1 | convolution fusion | flops 209976832 | bytes 3682312 | tf_op jit(solution)/shard_map/while/body/eval_jaxpr/dot_general | solution.py:70
  214.5 2.8 multiply_reduce_fusion.2
  223.1 3.3 %fusion.59 = (f32[512]{0:T(512)S(1)}, f32[512,1536]{1,0:T(8,128)S(1)}) fusion(f32[]{:T(128)} %bitcast.74, bf16[1536,256]{1,0:T(8,128)(2,1)} %get-tuple-element.625, s32[]{:T(128)S(6)} %select_n.97, bf16[512,1792]{1,0:T(8,128)(2,1)} %get-tuple-element.624, s32[]{:T(128)S(6)} %select_n.95, pred[1536]{0:T(1024)(128)(4,1)S(1)} %get-tuple-element.631, ...), kind=kOutput, calls=%fused_computation.80.clone.1 | convolution fusion | flops 209976832 | bytes 3682312 | tf_op jit(solution)/shard_map/while/body/eval_jaxpr/dot_general | solution.py:70
  227.8 2.8 multiply_reduce_fusion.2
  236.5 3.3 %fusion.59 = (f32[512]{0:T(512)S(1)}, f32[512,1536]{1,0:T(8,128)S(1)}) fusion(f32[]{:T(128)} %bitcast.74, bf16[1536,256]{1,0:T(8,128)(2,1)} %get-tuple-element.625, s32[]{:T(128)S(6)} %select_n.97, bf16[512,1792]{1,0:T(8,128)(2,1)} %get-tuple-element.624, s32[]{:T(128)S(6)} %select_n.95, pred[1536]{0:T(1024)(128)(4,1)S(1)} %get-tuple-element.631, ...), kind=kOutput, calls=%fused_computation.80.clone.1 | convolution fusion | flops 209976832 | bytes 3682312 | tf_op jit(solution)/shard_map/while/body/eval_jaxpr/dot_general | solution.py:70
  241.1 2.8 multiply_reduce_fusion.2
  249.8 3.3 %fusion.59 = (f32[512]{0:T(512)S(1)}, f32[512,1536]{1,0:T(8,128)S(1)}) fusion(f32[]{:T(128)} %bitcast.74, bf16[1536,256]{1,0:T(8,128)(2,1)} %get-tuple-element.625, s32[]{:T(128)S(6)} %select_n.97, bf16[512,1792]{1,0:T(8,128)(2,1)} %get-tuple-element.624, s32[]{:T(128)S(6)} %select_n.95, pred[1536]{0:T(1024)(128)(4,1)S(1)} %get-tuple-element.631, ...), kind=kOutput, calls=%fused_computation.80.clone.1 | convolution fusion | flops 209976832 | bytes 3682312 | tf_op jit(solution)/shard_map/while/body/eval_jaxpr/dot_general | solution.py:70
  254.4 2.8 multiply_reduce_fusion.2
  263.1 3.3 %fusion.59 = (f32[512]{0:T(512)S(1)}, f32[512,1536]{1,0:T(8,128)S(1)}) fusion(f32[]{:T(128)} %bitcast.74, bf16[1536,256]{1,0:T(8,128)(2,1)} %get-tuple-element.625, s32[]{:T(128)S(6)} %select_n.97, bf16[512,1792]{1,0:T(8,128)(2,1)} %get-tuple-element.624, s32[]{:T(128)S(6)} %select_n.95, pred[1536]{0:T(1024)(128)(4,1)S(1)} %get-tuple-element.631, ...), kind=kOutput, calls=%fused_computation.80.clone.1 | convolution fusion | flops 209976832 | bytes 3682312 | tf_op jit(solution)/shard_map/while/body/eval_jaxpr/dot_general | solution.py:70
  267.8 2.8 multiply_reduce_fusion.2
  276.1 1.9 collective-permute-start.3
  278.1 2.1 collective-permute-start.2
  280.1 11.2 %collective-permute-done.3 = bf16[2,512,256]{2,1,0:T(8,128)(2,1)S(1)} collective-permute-done((bf16[2,512,256]{2,1,0:T(8,128)(2,1)S(1)}, bf16[2,512,256]{2,1,0:T(8,128)(2,1)S(1)}, u32[]{:S(2)}, u32[]{:S(2)}) %collective-permute-start.3) | collective-permute-done | bytes 524320 | tf_op jit(solution)/shard_map/ppermute | solution.py:14
  291.3 5.9 %collective-permute-done.2 = bf16[2,512,256]{2,1,0:T(8,128)(2,1)S(1)} collective-permute-done((bf16[2,512,256]{2,1,0:T(8,128)(2,1)S(1)}, bf16[2,512,256]{2,1,0:T(8,128)(2,1)S(1)}, u32[]{:S(2)}, u32[]{:S(2)}) %collective-permute-start.2) | collective-permute-done | bytes 524320 | tf_op jit(solution)/shard_map/ppermute | solution.py:14
  (230 shorter events, 104.8 us)
Async XLA Ops:
  13.8 5.7 %copy-start.1 = (bf16[1,512,256]{2,1,0:T(8,128)(2,1)S(1)}, bf16[1,512,256]{2,1,0:T(8,128)(2,1)}, u32[]{:S(2)}) copy-start(bf16[1,512,256]{2,1,0:T(8,128)(2,1)} %param.11) | copy-start | bytes 786436
  13.8 6.4 %copy-start.2 = (bf16[1,512,256]{2,1,0:T(8,128)(2,1)S(1)}, bf16[1,512,256]{2,1,0:T(8,128)(2,1)}, u32[]{:S(2)}) copy-start(bf16[1,512,256]{2,1,0:T(8,128)(2,1)} %param.12) | copy-start | bytes 786436
  13.8 13.7 %copy-start.4 = (s32[1,512]{1,0:T(1,128)S(1)}, s32[1,512]{1,0:T(1,128)}, u32[]{:S(2)}) copy-start(s32[1,512]{1,0:T(1,128)} %param.16) | copy-start | bytes 6148
  13.8 72.2 %all-to-all-start = ((bf16[8,1,512,224]{2,3,1,0:T(8,128)(2,1)}), bf16[8,1,512,224]{2,3,1,0:T(8,128)(2,1)S(1)}, u32[]{:S(2)}, u32[]{:S(2)}) async-start(bf16[8,1,512,224]{2,3,1,0:T(8,128)(2,1)} %bitcast_dynamic-update-slice_fusion), calls=%async_computation | async-start | bytes 3670016 | tf_op jit(solution)/shard_map/all_to_all | solution.py:42
  20.9 63.7 %collective-permute-start.1 = (bf16[2,512,256]{2,1,0:T(8,128)(2,1)}, bf16[2,512,256]{2,1,0:T(8,128)(2,1)S(1)}, u32[]{:S(2)}, u32[]{:S(2)}) collective-permute-start(bf16[2,512,256]{2,1,0:T(8,128)(2,1)} %constant_dynamic-update-slice_fusion), channel_id=1, source_target_pairs={{0,1},{1,2},{2,3},{3,4},{4,5},{5,6},{6,7},{8,9},{9,10},{10,11},{11... | collective-permute-start | bytes 1572872 | tf_op jit(solution)/shard_map/ppermute | solution.py:14
  24.2 60.4 %collective-permute-start = (bf16[2,512,256]{2,1,0:T(8,128)(2,1)}, bf16[2,512,256]{2,1,0:T(8,128)(2,1)S(1)}, u32[]{:S(2)}, u32[]{:S(2)}) collective-permute-start(bf16[2,512,256]{2,1,0:T(8,128)(2,1)} %constant_dynamic-update-slice_fusion), channel_id=1, source_target_pairs={{0,2},{1,3},{2,4},{3,5},{4,6},{5,7},{8,10},{9,11},{10,12},{11,13},... | collective-permute-start | bytes 1572872 | tf_op jit(solution)/shard_map/ppermute | solution.py:14
  88.3 1.5 copy-start.5
  93.7 1.4 copy-start.3
  99.8 1.6 copy-start
  106.9 1.4 copy-start.3
  113.0 1.6 copy-start
  120.2 1.4 copy-start.3
  126.3 1.6 copy-start
  133.4 1.4 copy-start.3
  139.6 1.6 copy-start
  146.7 1.4 copy-start.3
  152.8 1.6 copy-start
  160.0 1.4 copy-start.3
  166.1 1.6 copy-start
  173.2 1.4 copy-start.3
  179.3 1.6 copy-start
  186.5 1.4 copy-start.3
  192.6 1.6 copy-start
  199.8 1.4 copy-start.3
  205.9 1.6 copy-start
  213.1 1.4 copy-start.3
  219.2 1.6 copy-start
  226.4 1.4 copy-start.3
  232.5 1.6 copy-start
  239.7 1.4 copy-start.3
  245.9 1.6 copy-start
  253.1 1.4 copy-start.3
  259.2 1.6 copy-start
  266.4 1.4 copy-start.3
  272.5 1.6 copy-start
  276.1 15.3 %collective-permute-start.3 = (bf16[2,512,256]{2,1,0:T(8,128)(2,1)S(1)}, bf16[2,512,256]{2,1,0:T(8,128)(2,1)S(1)}, u32[]{:S(2)}, u32[]{:S(2)}) collective-permute-start(bf16[2,512,256]{2,1,0:T(8,128)(2,1)S(1)} %pad_maximum_fusion.3), channel_id=1, source_target_pairs={{2,0},{3,1},{4,2},{5,3},{6,4},{7,5},{10,8},{11,9},{12,10},{13,11},... | collective-permute-start | bytes 1572872 | tf_op jit(solution)/shard_map/ppermute | solution.py:14
  278.1 19.2 %collective-permute-start.2 = (bf16[2,512,256]{2,1,0:T(8,128)(2,1)S(1)}, bf16[2,512,256]{2,1,0:T(8,128)(2,1)S(1)}, u32[]{:S(2)}, u32[]{:S(2)}) collective-permute-start(bf16[2,512,256]{2,1,0:T(8,128)(2,1)S(1)} %pad_maximum_fusion.2), channel_id=1, source_target_pairs={{1,0},{2,1},{3,2},{4,3},{5,4},{6,5},{7,6},{9,8},{10,9},{11,10},{12... | collective-permute-start | bytes 1572872 | tf_op jit(solution)/shard_map/ppermute | solution.py:14
